TPU v7x, 32 devices: a whole 2x2x4 slice. The times are simulated.
32 devices in a mesh: seq: 8 (over z, x), tp: 4 (over y, core).
Axes of the slice: x: 2, y: 2, z: 4, core: 2. Of those that a mesh axis runs over, the one named last changes fastest.
Arguments:
- draft_q: bfloat16 [256, 4096], P('seq', 'tp'), may hold values from -16 to 16
- draft_kv: bfloat16 [2, 256, 4096], P(None, 'seq', 'tp'), may hold values from -6 to 6
- kv_pool: bfloat16 [2, 128, 128, 4096], P(None, 'seq', None, 'tp'), may hold values from -8 to 8
- page_table: int32 [4, 32], replicated, may hold values from -1 to 127, as said below
- cache_len: int32 [4], replicated, may hold values from 2048 to 4096, as said below
- tree_mask: int32 [4, 64, 64], replicated, may hold values from 0 to 1, as said below
- accepted_rows: int32 [4, 64], replicated, may hold values from -1 to 63, as said below
- out_weight: bfloat16 [4096, 4096], P('tp'), may hold values from -0.125 to 0.125
Outputs:
- layer_out: bfloat16 [256, 4096], P('seq', 'tp')
- accepted_kv: bfloat16 [2, 4, 128, 4096], P(None, None, None, 'tp')
Inputs may be any that keep to these rules, and one draw needn't show every extreme that they name: `page_table`: entries past a request's cached pages are -1; the slots in use are distinct over all requests. `cache_len`: some request holds exactly 4096 cached tokens. `tree_mask`: entry (r, i, k) is 1 where draft row k is row i itself or one of its ancestors in request r's token tree; a parent precedes its children, row 0 is the root. `accepted_rows`: each row lists in ascending order the draft rows of one root-to-node path of the tree, then -1.
All inputs are finite; a program needn't handle non-finite values.
Results may differ from a plain program's by a relative error of at most 0.0051.
Values may be sent and summed in bfloat16 or wider, within the bound.
A program may use at most 128 MiB of HBM per device.

v0:
```python
import math
import jax
import jax.numpy as jnp
from jax import lax
from jax.sharding import PartitionSpec as P

HD = 128
NEGATIVE = -1e30


def body(draft_q, draft_kv, kv_pool, page_table, cache_len, tree_mask, accepted_rows, out_weight):
    inv_root = 1.0 / math.sqrt(HD)
    highest = lax.Precision.HIGHEST
    n_seq = lax.axis_size("seq")
    rows_dev = draft_q.shape[0]
    width_loc = draft_q.shape[1]
    heads_loc = width_loc // HD
    n_req = page_table.shape[0]
    n_pages = page_table.shape[1]
    n_draft = tree_mask.shape[1]
    n_slots = kv_pool.shape[1]
    page_len = kv_pool.shape[2]
    rows_all = rows_dev * n_seq
    query_all, kv_all = (
        lax.all_gather(draft_q, "seq", axis=0, tiled=True),
        lax.all_gather(draft_kv, "seq", axis=1, tiled=True),
    )
    first_slot = lax.axis_index("seq") * n_slots
    slot_ids = first_slot + jnp.arange(n_slots, dtype=jnp.int32)
    slot_hits = page_table[None, :, :] == slot_ids[:, None, None]
    owner_hot = jnp.any(slot_hits, axis=2)
    is_live = jnp.any(owner_hot, axis=1)
    owner_req = jnp.sum(owner_hot * jnp.arange(n_req, dtype=jnp.int32)[None, :], axis=1)
    logical = jnp.sum(slot_hits * jnp.arange(n_pages, dtype=jnp.int32)[None, None, :], axis=(1, 2))
    len_limit = jnp.sum(owner_hot * cache_len[None, :], axis=1)
    positions = logical[:, None] * page_len + jnp.arange(page_len, dtype=jnp.int32)[None, :]
    is_valid = is_live[:, None] & (positions < len_limit[:, None])
    query_req = query_all.reshape(n_req, n_draft, heads_loc, HD)
    page_query = query_req[owner_req]
    page_keys = kv_pool[0].reshape(n_slots, page_len, heads_loc, HD)
    page_values = kv_pool[1].reshape(n_slots, page_len, heads_loc, HD)
    scores = (
        jnp.einsum("sqhd,sthd->shqt", page_query, page_keys, preferred_element_type=jnp.float32)
        * inv_root
    )
    allowed = is_valid[:, None, None, :]
    masked = jnp.where(allowed, scores, NEGATIVE)
    page_max = jnp.max(masked, axis=3)
    weights = jnp.where(allowed, jnp.exp(masked - page_max[..., None]), 0.0)
    page_total = jnp.sum(weights, axis=3)
    page_out = jnp.einsum(
        "shqt,sthd->shqd",
        weights.astype(jnp.bfloat16),
        page_values,
        preferred_element_type=jnp.float32,
    )
    req_max = jnp.max(
        jnp.where(owner_hot[:, :, None, None], page_max[:, None, :, :], NEGATIVE), axis=0
    )
    weight = jnp.exp(page_max - req_max[owner_req])
    own_hot = owner_hot.astype(jnp.float32)
    local_total = jnp.einsum(
        "sr,shq->rqh", own_hot, weight * page_total, precision=highest
    ).reshape(rows_all, heads_loc)
    local_out = jnp.einsum(
        "sr,shqd->rqhd", own_hot, weight[..., None] * page_out, precision=highest
    ).reshape(rows_all, width_loc)
    local_max = jnp.transpose(req_max, (0, 2, 1)).reshape(rows_all, heads_loc)
    row_start = lax.axis_index("seq") * rows_dev
    got_max, got_total, got_out = (
        lax.all_to_all(local_max, "seq", split_axis=0, concat_axis=0, tiled=True),
        lax.all_to_all(local_total, "seq", split_axis=0, concat_axis=0, tiled=True),
        lax.all_to_all(local_out, "seq", split_axis=0, concat_axis=0, tiled=True),
    )
    got_max = got_max.reshape(n_seq, rows_dev, heads_loc)
    own_max = jnp.max(got_max, axis=0)
    factor = jnp.exp(got_max - own_max[None])
    own_total = jnp.sum(got_total.reshape(n_seq, rows_dev, heads_loc) * factor, axis=0)
    own_out = jnp.sum(got_out.reshape(n_seq, rows_dev, heads_loc, HD) * factor[..., None], axis=0)
    own_query = draft_q.reshape(rows_dev, heads_loc, HD)
    tree_keys = kv_all[0].reshape(rows_all, heads_loc, HD)
    tree_values = kv_all[1].reshape(rows_all, heads_loc, HD)
    ancestry = tree_mask.reshape(rows_all, n_draft)
    own_ancestry = lax.dynamic_slice_in_dim(ancestry, row_start, rows_dev, 0)
    row_req = (row_start + jnp.arange(rows_dev, dtype=jnp.int32)) // n_draft
    key_req = jnp.arange(rows_all, dtype=jnp.int32) // n_draft
    tree_allowed = (jnp.tile(own_ancestry, (1, n_req)) == 1) & (
        row_req[:, None] == key_req[None, :]
    )
    tree_scores = (
        jnp.einsum("qhd,khd->hqk", own_query, tree_keys, preferred_element_type=jnp.float32)
        * inv_root
    )
    tree_masked = jnp.where(tree_allowed[None], tree_scores, NEGATIVE)
    tree_max = jnp.max(tree_masked, axis=2)
    tree_weights = jnp.where(tree_allowed[None], jnp.exp(tree_masked - tree_max[..., None]), 0.0)
    tree_total = jnp.transpose(jnp.sum(tree_weights, axis=2))
    tree_out = jnp.einsum(
        "hqk,khd->qhd",
        tree_weights.astype(jnp.bfloat16),
        tree_values,
        preferred_element_type=jnp.float32,
    )
    tree_max = jnp.transpose(tree_max)
    row_top = jnp.maximum(own_max, tree_max)
    cache_factor = jnp.exp(own_max - row_top)
    tree_factor = jnp.exp(tree_max - row_top)
    numerator = own_out * cache_factor[..., None] + tree_out * tree_factor[..., None]
    denominator = own_total * cache_factor + tree_total * tree_factor
    attention = (
        (numerator / denominator[..., None]).reshape(rows_dev, width_loc).astype(jnp.bfloat16)
    )
    partial_value = jnp.dot(attention, out_weight, preferred_element_type=jnp.float32)
    layer_out = lax.psum_scatter(partial_value, "tp", scatter_dimension=1, tiled=True).astype(
        jnp.bfloat16
    )
    picked = jnp.concatenate(
        [accepted_rows, jnp.full((n_req, page_len - n_draft), -1, jnp.int32)], axis=1
    )
    onehot = (picked[:, :, None] == jnp.arange(n_draft, dtype=jnp.int32)[None, None, :]).astype(
        jnp.bfloat16
    )
    kv_blocks = kv_all.reshape(2, n_req, n_draft, width_loc)
    accepted_kv = jnp.einsum(
        "rji,crid->crjd", onehot, kv_blocks, preferred_element_type=jnp.float32
    ).astype(jnp.bfloat16)
    return (layer_out, accepted_kv)


def solution(mesh):
    return jax.shard_map(
        body,
        mesh=mesh,
        in_specs=(
            P("seq", "tp"),
            P(None, "seq", "tp"),
            P(None, "seq", None, "tp"),
            P(),
            P(),
            P(),
            P(),
            P("tp", None),
        ),
        out_specs=(P("seq", "tp"), P(None, None, None, "tp")),
        check_vma=False,
    )
```

profile of v0, /device:TPU:0, one launch (start us, length us, event | category | flops | bytes accessed | tf_op | source)
XLA Modules:
  0.0 172.4 jit_solution(13782191911061992662)
XLA Ops:
  7.2 1.0 compare_reduce_fusion.1
  9.9 33.2 %all_gather.6 = bf16[256,1024]{1,0:T(8,128)(2,1)S(1)} all-gather(bf16[32,1024]{1,0:T(8,128)(2,1)} %param.8), channel_id=1, replica_groups=mesh['seq'=8,'tp'=4] {'seq'}, dimensions={0}, use_global_device_ids=true | all-gather | bytes 589824 | tf_op jit(solution)/shard_map/all_gather | solution.py:25
  43.2 6.0 %fusion.53 = (bf16[1,16,128,1024]{3,2,1,0:T(8,128)(2,1)}, bf16[1,16,128,1024]{3,2,1,0:T(8,128)(2,1)}) fusion(bf16[2,16,128,1024]{3,2,1,0:T(8,128)(2,1)} %param.10), kind=kLoop, calls=%fused_computation.86 | loop fusion | bytes 16777216 | tf_op jit(solution)/shard_map/slice | solution.py:40
  49.3 6.4 %copy.128 = bf16[1,16,128,1024]{2,3,1,0:T(8,128)(2,1)} copy(bf16[1,16,128,1024]{3,2,1,0:T(8,128)(2,1)} %get-tuple-element.25) | data formatting | bytes 8388608
  56.7 3.5 %fusion.2 = (f32[16,8,64]{2,1,0:T(8,128)S(1)}, f32[16,8,64,128]{3,2,1,0:T(8,128)S(1)}) fusion(pred[16,128]{1,0:T(8,128)(4,1)S(1)} %fusion.39, bf16[16,128,8,128]{1,3,2,0:T(8,128)(2,1)} %bitcast.99, bf16[16,64,8,128]{3,2,1,0:T(8,128)(2,1)S(1)} %gather_fusion), kind=kOutput, calls=%fused_computation.6 | convolution fusion | flops 271572992 | bytes 10520576 | tf_op jit(solution)/shard_map/sqhd,sthd->shqt/dot_general | solution.py:43
  60.2 1.9 %copy-done = f32[16,8,64,128]{3,2,1,0:T(8,128)} copy-done((f32[16,8,64,128]{3,2,1,0:T(8,128)}, f32[16,8,64,128]{3,2,1,0:T(8,128)S(1)}, u32[]{:S(2)}) %copy-start) | copy-done | bytes 4194328
  62.1 2.4 %fusion.3 = f32[16,8,64]{2,1,0:T(8,128)S(1)} fusion(f32[16,8,64,128]{3,2,1,0:T(8,128)S(1)} %get-tuple-element.30, f32[16,8,64]{2,1,0:T(8,128)S(1)} %get-tuple-element.29, pred[16,128]{1,0:T(8,128)(4,1)S(1)} %fusion.39), kind=kLoop, calls=%fused_computation.7 | loop fusion | flops 5234688 | bytes 4261888 | tf_op jit(solution)/shard_map/reduce_sum | solution.py:50
  66.2 5.7 %all-to-all-start.2 = ((f32[8,1,256]{2,1,0:T(1,128)}), f32[8,1,256]{2,1,0:T(1,128)S(1)}, u32[]{:S(2)}, u32[]{:S(2)}) async-start(f32[8,1,256]{2,1,0:T(1,128)} %reshape.220), calls=%async_computation.2 | async-start | bytes 16384 | tf_op jit(solution)/shard_map/all_to_all | solution.py:72
  72.8 6.4 %copy.129 = bf16[1,16,128,1024]{2,3,1,0:T(8,128)(2,1)} copy(bf16[1,16,128,1024]{3,2,1,0:T(8,128)(2,1)} %get-tuple-element.26) | data formatting | bytes 8388608
  79.1 6.6 %convolution_multiply_fusion = f32[16,8,64,128]{3,2,1,0:T(8,128)} fusion(bf16[16,128,8,128]{1,3,2,0:T(8,128)(2,1)} %bitcast.100, f32[16,8,64,128]{3,2,1,0:T(8,128)} %copy-done, f32[16,8,64]{2,1,0:T(8,128)S(1)} %get-tuple-element.29, f32[16,8,64]{2,1,0:T(8,128)S(1)} %get-tuple-element.24, pred[16,128]{1,0:T(8,128)(4,1)S(1)} %fusion.39), kind=kOutput, calls=%fused_computation.9 | convolution fusion | flops 274726912 | bytes 12650496 | tf_op jit(solution)/shard_map/shqt,sthd->shqd/dot_general | solution.py:51
  86.6 6.0 %all-to-all-start.1 = ((f32[8,1,256]{2,1,0:T(1,128)}), f32[8,1,256]{2,1,0:T(1,128)S(1)}, u32[]{:S(2)}, u32[]{:S(2)}) async-start(f32[8,1,256]{2,1,0:T(1,128)} %reshape.218), calls=%async_computation.1 | async-start | bytes 16384 | tf_op jit(solution)/shard_map/all_to_all | solution.py:71
  92.5 5.9 %fusion.13 = f32[4,64,8,128]{3,0,1,2:T(4,128)S(1)} fusion(f32[16,8,64,128]{3,2,1,0:T(8,128)} %convolution_multiply_fusion, pred[16,4]{0,1:T(4,128)(4,1)S(1)} %get-tuple-element.15), kind=kOutput, calls=%fused_computation.18 | convolution fusion | flops 50331648 | bytes 5242944 | tf_op jit(solution)/shard_map/sr,shqd->rqhd/dot_general | solution.py:65
  99.1 1.1 all_to_all.18
  100.2 6.0 %all-to-all-start = ((f32[8,32,1024]{2,1,0:T(8,128)}), f32[8,32,1024]{2,1,0:T(8,128)S(1)}, u32[]{:S(2)}, u32[]{:S(2)}) async-start(f32[8,32,1024]{2,1,0:T(8,128)} %all_to_all.18), calls=%async_computation | async-start | bytes 2097152 | tf_op jit(solution)/shard_map/all_to_all | solution.py:73
  110.0 13.2 %all-gather.2.cloned.1.call-done = bf16[2,256,1024]{2,0,1:T(2,128)(2,1)} async-done(((bf16[2,32,1024]{2,0,1:T(2,128)(2,1)}), bf16[2,256,1024]{2,0,1:T(2,128)(2,1)}) %all-gather.2.cloned.1.call-update) | async-done | bytes 1048592 | tf_op jit(solution)/shard_map/all_gather | solution.py:26
  123.2 4.1 %fusion.54 = (bf16[1,256,1024]{2,0,1:T(2,128)(2,1)}, bf16[1,256,1024]{2,0,1:T(2,128)(2,1)S(1)}) fusion(bf16[2,256,1024]{2,0,1:T(2,128)(2,1)} %all-gather.2.cloned.1.call-done), kind=kLoop, calls=%fused_computation.87 | loop fusion | bytes 2097152 | tf_op jit(solution)/shard_map/slice | solution.py:81
  127.3 3.5 %copy.130 = bf16[1,256,1024]{1,2,0:T(8,128)(2,1)} copy(bf16[1,256,1024]{2,0,1:T(2,128)(2,1)} %get-tuple-element.27) | data formatting | bytes 1048576
  130.8 2.0 %copy.131 = bf16[1,256,1024]{1,2,0:T(8,128)(2,1)} copy(bf16[1,256,1024]{2,0,1:T(2,128)(2,1)S(1)} %get-tuple-element.28) | data formatting | bytes 1048576
  132.8 1.3 fusion.55
  134.5 1.4 fusion.21
  135.9 5.8 %fusion.31 = f32[32,4096]{1,0:T(8,128)} fusion(bf16[1024,4096]{1,0:T(8,128)(2,1)} %param.15, bf16[8,4,8,128]{3,2,1,0:T(8,128)(2,1)S(1)} %fusion.21), kind=kOutput, calls=%fused_computation.40 | convolution fusion | flops 268435456 | bytes 8978432 | tf_op jit(solution)/shard_map/dot_general | solution.py:113
  142.6 1.5 copy.119
  144.0 20.0 %reduce-scatter.2.cloned.1.call-done = f32[32,1024]{1,0:T(8,128)} async-done(((f32[32,4096]{1,0:T(8,128)}), f32[32,1024]{1,0:T(8,128)}) %reduce-scatter.2.cloned.1.call-update) | async-done | bytes 131088 | tf_op jit(solution)/shard_map/reduce_scatter | solution.py:114
  164.0 1.5 convert_element_type.30
  (60 shorter events, 11.7 us)
Async XLA Ops:
  60.2 2.0 %copy-start = (f32[16,8,64,128]{3,2,1,0:T(8,128)}, f32[16,8,64,128]{3,2,1,0:T(8,128)S(1)}, u32[]{:S(2)}) copy-start(f32[16,8,64,128]{3,2,1,0:T(8,128)S(1)} %get-tuple-element.30) | copy-start | bytes 12582916
  60.2 11.8 %copy-start.3 = (bf16[2,32,1024]{2,1,0:T(8,128)(2,1)S(1)}, bf16[2,32,1024]{2,1,0:T(8,128)(2,1)}, u32[]{:S(2)}) copy-start(bf16[2,32,1024]{2,1,0:T(8,128)(2,1)} %param.9) | copy-start | bytes 393220
  66.2 20.3 %all-to-all-start.2 = ((f32[8,1,256]{2,1,0:T(1,128)}), f32[8,1,256]{2,1,0:T(1,128)S(1)}, u32[]{:S(2)}, u32[]{:S(2)}) async-start(f32[8,1,256]{2,1,0:T(1,128)} %reshape.220), calls=%async_computation.2 | async-start | bytes 16384 | tf_op jit(solution)/shard_map/all_to_all | solution.py:72
  71.9 51.4 %all-gather.2.cloned.1.call-start = ((), (), s32[]{:S(2)}) async-start(), calls=%async_computation.4 | async-start | bytes 1179648 | tf_op jit(solution)/shard_map/all_gather | solution.py:26
  86.6 13.7 %all-to-all-start.1 = ((f32[8,1,256]{2,1,0:T(1,128)}), f32[8,1,256]{2,1,0:T(1,128)S(1)}, u32[]{:S(2)}, u32[]{:S(2)}) async-start(f32[8,1,256]{2,1,0:T(1,128)} %reshape.218), calls=%async_computation.1 | async-start | bytes 16384 | tf_op jit(solution)/shard_map/all_to_all | solution.py:71
  100.2 34.1 %all-to-all-start = ((f32[8,32,1024]{2,1,0:T(8,128)}), f32[8,32,1024]{2,1,0:T(8,128)S(1)}, u32[]{:S(2)}, u32[]{:S(2)}) async-start(f32[8,32,1024]{2,1,0:T(8,128)} %all_to_all.18), calls=%async_computation | async-start | bytes 2097152 | tf_op jit(solution)/shard_map/all_to_all | solution.py:73
  106.2 57.8 %reduce-scatter.2.cloned.1.call-start = ((), (), s32[]{:S(2)}) async-start(), calls=%async_computation.5 | async-start | bytes 655360 | tf_op jit(solution)/shard_map/reduce_scatter | solution.py:114
  110.0 22.8 %copy-start.2 = (bf16[32,1024]{1,0:T(8,128)(2,1)S(1)}, bf16[32,1024]{1,0:T(8,128)(2,1)}, u32[]{:S(2)}) copy-start(bf16[32,1024]{1,0:T(8,128)(2,1)} %param.8) | copy-start | bytes 196612
  135.9 5.9 %copy-start.4 = (s32[4,64]{1,0:T(4,128)S(1)}, s32[4,64]{1,0:T(4,128)}, u32[]{:S(2)}) copy-start(s32[4,64]{1,0:T(4,128)} %param.14) | copy-start | bytes 3076
  135.9 5.9 %copy-start.1 = (bf16[2,256,1024]{2,0,1:T(2,128)(2,1)S(1)}, bf16[2,256,1024]{2,0,1:T(2,128)(2,1)}, u32[]{:S(2)}) copy-start(bf16[2,256,1024]{2,0,1:T(2,128)(2,1)} %all-gather.2.cloned.1.call-done) | copy-start | bytes 3145732
Sparse Core Ops, SparseCore 0:
  75.4 47.7 all-gather.1
  141.9 22.0 reduce-scatter.1
where the time goes:
time: 173 us; the launch traced here: 172 us
  local copies, waits for them, and re-layouts  38.9 us (22%)
  blocking collectives  33.2 us (19%)
  waiting for transfers between devices  33.2 us (19%)
  matrix products  25.5 us (15%)
  starting transfers between devices  17.8 us (10%)
  between operations  14.3 us (8%)
  other arithmetic  9.37 us (5%)
    all_gather x1, blocking collectives, body(): lax.all_gather(draft_q, 'seq', axis=0, tiled=True)  33.2 us
    unnamed x21, local copies, waits for them, and re-layouts  24 us
    reduce_scatter x1, waiting for transfers between devices, body(): lax.psum_scatter(partial_value, 'tp', scatter_dimension=1, tiled=True)  20 us
    all_gather x1, waiting for transfers between devices, body(): lax.all_gather(draft_kv, 'seq', axis=1, tiled=True)  13.2 us
    dot_general x1, matrix products, body(): jnp.einsum('shqt,sthd->shqd', weights.astype(jnp.bfloat16), page_values,...  6.64 us
    slice x1, local copies, waits for them, and re-layouts, body(): page_keys = kv_pool[0].reshape(n_slots, page_len, heads_loc, HD)  6.01 us
    all_to_all x1, starting transfers between devices, body(): lax.all_to_all(local_out, 'seq', split_axis=0, concat_axis=0, tiled=True)  5.98 us
    all_to_all x1, starting transfers between devices, body(): lax.all_to_all(local_max, 'seq', split_axis=0, concat_axis=0, tiled=True)  5.95 us
  transfers between devices with their start and end apart: 5, of which 2 were waited for; matrix products, arithmetic and copies ran while one was open for 22% of the time, Pallas kernels for 0%

commit v1 on v0

--- a/solution.py
+++ b/solution.py
@@ -6,6 +6,27 @@
 
 HD = 128
 NEGATIVE = -1e30
+
+
+def joined_along(tiles, dim):
+    lengths = list(tiles.shape[1:])
+    lengths[dim] *= tiles.shape[0]
+    return jnp.moveaxis(tiles, 0, dim).reshape(lengths)
+
+
+def grow_blocks(value, axis):
+    size, mine = (lax.axis_size(axis), lax.axis_index(axis))
+    blocks, bit = (value[None], 1)
+    while bit < size:
+        other = lax.ppermute(blocks, axis, [(i, i ^ bit) for i in range(size)])
+        low = mine & bit == 0
+        blocks = jnp.concatenate([jnp.where(low, blocks, other), jnp.where(low, other, blocks)])
+        bit *= 2
+    return blocks
+
+
+def gather_by_bits(x, axis, dim):
+    return joined_along(grow_blocks(x, axis), dim)
 
 
 def body(draft_q, draft_kv, kv_pool, page_table, cache_len, tree_mask, accepted_rows, out_weight):
@@ -22,7 +43,7 @@
     page_len = kv_pool.shape[2]
     rows_all = rows_dev * n_seq
     query_all, kv_all = (
-        lax.all_gather(draft_q, "seq", axis=0, tiled=True),
+        gather_by_bits(draft_q, "seq", 0),
         lax.all_gather(draft_kv, "seq", axis=1, tiled=True),
     )
     first_slot = lax.axis_index("seq") * n_slots

time: 173 us -> 147 us (0.85)
  blocking collectives: 33.2 us -> 0 us
  starting transfers between devices: 17.8 us -> 23.3 us
    all_gather x1 -> x0, blocking collectives: 33.2 us -> none  [body(): lax.all_gather(draft_q, 'seq', axis=0, tiled=True)]
    all_gather x1, waiting for transfers between devices: 13.2 us -> 0.02 us  [body(): lax.all_gather(draft_kv, 'seq', axis=1, tiled=True)]
    all_to_all x1, waiting for transfers between devices: 0.01 us -> 10.1 us  [body(): lax.all_to_all(local_out, 'seq', split_axis=0, concat_axis=0, tiled=True)]
    ppermute x0 -> x3, starting transfers between devices: none -> 7.27 us  [grow_blocks(): other = lax.ppermute(blocks, axis, [(i, i ^ bit) for i in range(size)])]
    ppermute x0 -> x3, waiting for transfers between devices: none -> 5.3 us  [grow_blocks(): other = lax.ppermute(blocks, axis, [(i, i ^ bit) for i in range(size)])]
    all_to_all x1, starting transfers between devices: 5.66 us -> 3.75 us  [body(): lax.all_to_all(local_total, 'seq', split_axis=0, concat_axis=0, tiled=True)]
  transfers between devices with their start and end apart: 5 -> 8, of which waited for: 2 -> 4; matrix products, arithmetic and copies ran while one was open for 22% -> 43% of each run, Pallas kernels for 0% -> 0%
where the time goes in v1:
time: 147 us; the launch traced here: 146 us
  local copies, waits for them, and re-layouts  39.9 us (27%)
  waiting for transfers between devices  33.9 us (23%)
  matrix products  25.5 us (17%)
  starting transfers between devices  23.3 us (16%)
  between operations  14.4 us (10%)
  other arithmetic  8.86 us (6%)
    unnamed x21, local copies, waits for them, and re-layouts  25 us
    reduce_scatter x1, waiting for transfers between devices, body(): lax.psum_scatter(partial_value, 'tp', scatter_dimension=1, tiled=True)  18.5 us
    all_to_all x1, waiting for transfers between devices, body(): lax.all_to_all(local_out, 'seq', split_axis=0, concat_axis=0, tiled=True)  10.1 us
    ppermute x3, starting transfers between devices, grow_blocks(): other = lax.ppermute(blocks, axis, [(i, i ^ bit) for i in range(size)])  7.27 us
    dot_general x1, matrix products, body(): jnp.einsum('shqt,sthd->shqd', weights.astype(jnp.bfloat16), page_values,...  6.65 us
    slice x1, local copies, waits for them, and re-layouts, body(): page_keys = kv_pool[0].reshape(n_slots, page_len, heads_loc, HD)  6.09 us
    all_to_all x1, starting transfers between devices, body(): lax.all_to_all(local_out, 'seq', split_axis=0, concat_axis=0, tiled=True)  6 us
    all_to_all x1, starting transfers between devices, body(): lax.all_to_all(local_max, 'seq', split_axis=0, concat_axis=0, tiled=True)  5.99 us
  transfers between devices with their start and end apart: 8, of which 4 were waited for; matrix products, arithmetic and copies ran while one was open for 43% of the time, Pallas kernels for 0%

profile of v1, /device:TPU:0, one launch (start us, length us, event | category | flops | bytes accessed | tf_op | source)
XLA Modules:
  0.0 145.8 jit_solution(12775370423795322277)
XLA Ops:
  7.2 3.0 %collective-permute-start = (bf16[1,32,1024]{2,1,0:T(8,128)(2,1)}, bf16[1,32,1024]{2,1,0:T(8,128)(2,1)S(1)}, u32[]{:S(2)}, u32[]{:S(2)}) collective-permute-start(bf16[1,32,1024]{2,1,0:T(8,128)(2,1)} %bitcast.111), channel_id=1, source_target_pairs={{0,4},{4,0},{8,12},{12,8},{16,20},{20,16},{24,28},{28,24},{1,5},{5... | collective-permute-start | bytes 196616 | tf_op jit(solution)/shard_map/ppermute | solution.py:21
  10.2 1.7 %copy.107 = bf16[2,32,1024]{2,0,1:T(2,128)(2,1)} copy(bf16[2,32,1024]{2,1,0:T(8,128)(2,1)} %param.9) | data formatting | bytes 262144 | tf_op args[1]
  13.7 6.1 %fusion.53 = (bf16[1,16,128,1024]{3,2,1,0:T(8,128)(2,1)}, bf16[1,16,128,1024]{3,2,1,0:T(8,128)(2,1)}) fusion(bf16[2,16,128,1024]{3,2,1,0:T(8,128)(2,1)} %param.10), kind=kLoop, calls=%fused_computation.95 | loop fusion | bytes 16777216 | tf_op jit(solution)/shard_map/slice | solution.py:61
  20.1 1.6 %collective-permute-start.1 = (bf16[2,32,1024]{2,1,0:T(8,128)(2,1)S(1)}, bf16[2,32,1024]{2,1,0:T(8,128)(2,1)S(1)}, u32[]{:S(2)}, u32[]{:S(2)}) collective-permute-start(bf16[2,32,1024]{2,1,0:T(8,128)(2,1)S(1)} %pad_maximum_fusion.2), channel_id=1, source_target_pairs={{0,8},{4,12},{8,0},{12,4},{16,24},{20,28},{24,16},{28,20},{1,9},{5... | collective-permute-start | bytes 393224 | tf_op jit(solution)/shard_map/ppermute | solution.py:21
  21.7 4.8 %collective-permute-done.1 = bf16[2,32,1024]{2,1,0:T(8,128)(2,1)S(1)} collective-permute-done((bf16[2,32,1024]{2,1,0:T(8,128)(2,1)S(1)}, bf16[2,32,1024]{2,1,0:T(8,128)(2,1)S(1)}, u32[]{:S(2)}, u32[]{:S(2)}) %collective-permute-start.1) | collective-permute-done | bytes 131104 | tf_op jit(solution)/shard_map/ppermute | solution.py:21
  26.6 2.6 %collective-permute-start.2 = (bf16[4,32,1024]{2,1,0:T(8,128)(2,1)S(1)}, bf16[4,32,1024]{2,1,0:T(8,128)(2,1)S(1)}, u32[]{:S(2)}, u32[]{:S(2)}) collective-permute-start(bf16[4,32,1024]{2,1,0:T(8,128)(2,1)S(1)} %pad_maximum_fusion.1), channel_id=1, source_target_pairs={{0,16},{4,20},{8,24},{12,28},{16,0},{20,4},{24,8},{28,12},{1,17},{... | collective-permute-start | bytes 786440 | tf_op jit(solution)/shard_map/ppermute | solution.py:21
  29.3 6.4 %copy.128 = bf16[1,16,128,1024]{2,3,1,0:T(8,128)(2,1)} copy(bf16[1,16,128,1024]{3,2,1,0:T(8,128)(2,1)} %get-tuple-element.25) | data formatting | bytes 8388608
  35.7 6.4 %copy.129 = bf16[1,16,128,1024]{2,3,1,0:T(8,128)(2,1)} copy(bf16[1,16,128,1024]{3,2,1,0:T(8,128)(2,1)} %get-tuple-element.26) | data formatting | bytes 8388608
  43.8 3.5 %fusion.2 = (f32[16,8,64]{2,1,0:T(8,128)S(1)}, f32[16,8,64,128]{3,2,1,0:T(8,128)S(1)}) fusion(pred[16,128]{1,0:T(8,128)(4,1)S(1)} %fusion.39, bf16[16,128,8,128]{1,3,2,0:T(8,128)(2,1)} %bitcast.104, bf16[16,64,8,128]{3,2,1,0:T(8,128)(2,1)S(1)} %gather_fusion), kind=kOutput, calls=%fused_computation.6 | convolution fusion | flops 271572992 | bytes 10520576 | tf_op jit(solution)/shard_map/sqhd,sthd->shqt/dot_general | solution.py:64
  47.3 2.0 %copy-done = f32[16,8,64,128]{3,2,1,0:T(8,128)} copy-done((f32[16,8,64,128]{3,2,1,0:T(8,128)}, f32[16,8,64,128]{3,2,1,0:T(8,128)S(1)}, u32[]{:S(2)}) %copy-start) | copy-done | bytes 4194328
  49.3 2.4 %fusion.3 = f32[16,8,64]{2,1,0:T(8,128)S(1)} fusion(f32[16,8,64,128]{3,2,1,0:T(8,128)S(1)} %get-tuple-element.36, f32[16,8,64]{2,1,0:T(8,128)S(1)} %get-tuple-element.35, pred[16,128]{1,0:T(8,128)(4,1)S(1)} %fusion.39), kind=kLoop, calls=%fused_computation.7 | loop fusion | flops 5234688 | bytes 4261888 | tf_op jit(solution)/shard_map/reduce_sum | solution.py:71
  53.4 3.8 %all-to-all-start.2 = ((f32[8,1,256]{2,1,0:T(1,128)}), f32[8,1,256]{2,1,0:T(1,128)S(1)}, u32[]{:S(2)}, u32[]{:S(2)}) async-start(f32[8,1,256]{2,1,0:T(1,128)} %reshape.216), calls=%async_computation.2 | async-start | bytes 16384 | tf_op jit(solution)/shard_map/all_to_all | solution.py:93
  57.1 6.6 %convolution_multiply_fusion = f32[16,8,64,128]{3,2,1,0:T(8,128)} fusion(bf16[16,128,8,128]{1,3,2,0:T(8,128)(2,1)} %bitcast.103, f32[16,8,64,128]{3,2,1,0:T(8,128)} %copy-done, f32[16,8,64]{2,1,0:T(8,128)S(1)} %get-tuple-element.35, f32[16,8,64]{2,1,0:T(8,128)S(1)} %get-tuple-element.24, pred[16,128]{1,0:T(8,128)(4,1)S(1)} %fusion.39), kind=kOutput, calls=%fused_computation.9 | convolution fusion | flops 274726912 | bytes 12650496 | tf_op jit(solution)/shard_map/shqt,sthd->shqd/dot_general | solution.py:72
  64.5 6.0 %all-to-all-start.1 = ((f32[8,1,256]{2,1,0:T(1,128)}), f32[8,1,256]{2,1,0:T(1,128)S(1)}, u32[]{:S(2)}, u32[]{:S(2)}) async-start(f32[8,1,256]{2,1,0:T(1,128)} %reshape.214), calls=%async_computation.1 | async-start | bytes 16384 | tf_op jit(solution)/shard_map/all_to_all | solution.py:92
  70.5 5.9 %fusion.13 = f32[4,64,8,128]{3,0,1,2:T(4,128)S(1)} fusion(f32[16,8,64,128]{3,2,1,0:T(8,128)} %convolution_multiply_fusion, pred[16,4]{0,1:T(4,128)(4,1)S(1)} %get-tuple-element.15), kind=kOutput, calls=%fused_computation.18 | convolution fusion | flops 50331648 | bytes 5242944 | tf_op jit(solution)/shard_map/sr,shqd->rqhd/dot_general | solution.py:86
  78.2 6.0 %all-to-all-start = ((f32[8,32,1024]{2,1,0:T(8,128)}), f32[8,32,1024]{2,1,0:T(8,128)S(1)}, u32[]{:S(2)}, u32[]{:S(2)}) async-start(f32[8,32,1024]{2,1,0:T(8,128)} %all_to_all.18), calls=%async_computation | async-start | bytes 2097152 | tf_op jit(solution)/shard_map/all_to_all | solution.py:94
  88.1 4.1 %fusion.54 = (bf16[1,256,1024]{2,0,1:T(2,128)(2,1)}, bf16[1,256,1024]{2,0,1:T(2,128)(2,1)S(1)}) fusion(bf16[2,256,1024]{2,0,1:T(2,128)(2,1)} %all-gather.2.cloned.1.call-done), kind=kLoop, calls=%fused_computation.96 | loop fusion | bytes 2097152 | tf_op jit(solution)/shard_map/slice | solution.py:102
  92.2 3.5 %copy.130 = bf16[1,256,1024]{1,2,0:T(8,128)(2,1)} copy(bf16[1,256,1024]{2,0,1:T(2,128)(2,1)} %get-tuple-element.27) | data formatting | bytes 1048576
  95.7 2.0 %copy.131 = bf16[1,256,1024]{1,2,0:T(8,128)(2,1)} copy(bf16[1,256,1024]{2,0,1:T(2,128)(2,1)S(1)} %get-tuple-element.28) | data formatting | bytes 1048576
  99.2 10.1 %all-to-all-done = f32[8,32,1024]{2,1,0:T(8,128)S(1)} async-done(((f32[8,32,1024]{2,1,0:T(8,128)}), f32[8,32,1024]{2,1,0:T(8,128)S(1)}, u32[]{:S(2)}, u32[]{:S(2)}) %all-to-all-start) | async-done | bytes 1048608 | tf_op jit(solution)/shard_map/all_to_all | solution.py:94
  110.9 5.8 %fusion.31 = f32[32,4096]{1,0:T(8,128)} fusion(bf16[1024,4096]{1,0:T(8,128)(2,1)} %param.15, bf16[8,4,8,128]{3,2,1,0:T(8,128)(2,1)S(1)} %fusion.21), kind=kOutput, calls=%fused_computation.47 | convolution fusion | flops 268435456 | bytes 8978432 | tf_op jit(solution)/shard_map/dot_general | solution.py:134
  117.5 1.5 %copy.119 = bf16[2,4,128,1024]{3,2,1,0:T(8,128)(2,1)} copy(bf16[2,4,128,1024]{3,2,0,1:T(8,128)(2,1)S(1)} %convert_bitcast_fusion) | data formatting | bytes 4194304
  119.0 18.5 %reduce-scatter.2.cloned.1.call-done = f32[32,1024]{1,0:T(8,128)} async-done(((f32[32,4096]{1,0:T(8,128)}), f32[32,1024]{1,0:T(8,128)}) %reduce-scatter.2.cloned.1.call-update) | async-done | bytes 131088 | tf_op jit(solution)/shard_map/reduce_scatter | solution.py:135
  137.4 1.5 %convert_element_type.30 = bf16[32,1024]{1,0:T(8,128)(2,1)} convert(f32[32,1024]{1,0:T(8,128)} %reduce-scatter.2.cloned.1.call-done) | non-fusion elementwise | flops 32768 | bytes 196608 | tf_op jit(solution)/shard_map/convert_element_type | solution.py:135
  (71 shorter events, 15.7 us)
Async XLA Ops:
  7.2 80.9 %all-gather.2.cloned.1.call-start = ((), (), s32[]{:S(2)}) async-start(), calls=%async_computation.4 | async-start | bytes 1179648 | tf_op jit(solution)/shard_map/all_gather | solution.py:47
  7.2 12.8 %collective-permute-start = (bf16[1,32,1024]{2,1,0:T(8,128)(2,1)}, bf16[1,32,1024]{2,1,0:T(8,128)(2,1)S(1)}, u32[]{:S(2)}, u32[]{:S(2)}) collective-permute-start(bf16[1,32,1024]{2,1,0:T(8,128)(2,1)} %bitcast.111), channel_id=1, source_target_pairs={{0,4},{4,0},{8,12},{12,8},{16,20},{20,16},{24,28},{28,24},{1,5},{5... | collective-permute-start | bytes 196616 | tf_op jit(solution)/shard_map/ppermute | solution.py:21
  13.7 6.1 %copy-start.3 = (s32[4,32]{1,0:T(4,128)S(1)}, s32[4,32]{1,0:T(4,128)}, u32[]{:S(2)}) copy-start(s32[4,32]{1,0:T(4,128)} %param.11) | copy-start | bytes 1540
  13.7 6.3 %copy-start.2 = (bf16[32,1024]{1,0:T(8,128)(2,1)S(1)}, bf16[32,1024]{1,0:T(8,128)(2,1)}, u32[]{:S(2)}) copy-start(bf16[32,1024]{1,0:T(8,128)(2,1)} %param.8) | copy-start | bytes 196612
  20.1 6.5 %collective-permute-start.1 = (bf16[2,32,1024]{2,1,0:T(8,128)(2,1)S(1)}, bf16[2,32,1024]{2,1,0:T(8,128)(2,1)S(1)}, u32[]{:S(2)}, u32[]{:S(2)}) collective-permute-start(bf16[2,32,1024]{2,1,0:T(8,128)(2,1)S(1)} %pad_maximum_fusion.2), channel_id=1, source_target_pairs={{0,8},{4,12},{8,0},{12,4},{16,24},{20,28},{24,16},{28,20},{1,9},{5... | collective-permute-start | bytes 393224 | tf_op jit(solution)/shard_map/ppermute | solution.py:21
  26.6 16.0 %collective-permute-start.2 = (bf16[4,32,1024]{2,1,0:T(8,128)(2,1)S(1)}, bf16[4,32,1024]{2,1,0:T(8,128)(2,1)S(1)}, u32[]{:S(2)}, u32[]{:S(2)}) collective-permute-start(bf16[4,32,1024]{2,1,0:T(8,128)(2,1)S(1)} %pad_maximum_fusion.1), channel_id=1, source_target_pairs={{0,16},{4,20},{8,24},{12,28},{16,0},{20,4},{24,8},{28,12},{1,17},{... | collective-permute-start | bytes 786440 | tf_op jit(solution)/shard_map/ppermute | solution.py:21
  47.3 2.0 %copy-start = (f32[16,8,64,128]{3,2,1,0:T(8,128)}, f32[16,8,64,128]{3,2,1,0:T(8,128)S(1)}, u32[]{:S(2)}) copy-start(f32[16,8,64,128]{3,2,1,0:T(8,128)S(1)} %get-tuple-element.36) | copy-start | bytes 12582916
  53.4 11.2 %all-to-all-start.2 = ((f32[8,1,256]{2,1,0:T(1,128)}), f32[8,1,256]{2,1,0:T(1,128)S(1)}, u32[]{:S(2)}, u32[]{:S(2)}) async-start(f32[8,1,256]{2,1,0:T(1,128)} %reshape.216), calls=%async_computation.2 | async-start | bytes 16384 | tf_op jit(solution)/shard_map/all_to_all | solution.py:93
  64.5 13.7 %all-to-all-start.1 = ((f32[8,1,256]{2,1,0:T(1,128)}), f32[8,1,256]{2,1,0:T(1,128)S(1)}, u32[]{:S(2)}, u32[]{:S(2)}) async-start(f32[8,1,256]{2,1,0:T(1,128)} %reshape.214), calls=%async_computation.1 | async-start | bytes 16384 | tf_op jit(solution)/shard_map/all_to_all | solution.py:92
  78.2 31.1 %all-to-all-start = ((f32[8,32,1024]{2,1,0:T(8,128)}), f32[8,32,1024]{2,1,0:T(8,128)S(1)}, u32[]{:S(2)}, u32[]{:S(2)}) async-start(f32[8,32,1024]{2,1,0:T(8,128)} %all_to_all.18), calls=%async_computation | async-start | bytes 2097152 | tf_op jit(solution)/shard_map/all_to_all | solution.py:94
  84.2 53.2 %reduce-scatter.2.cloned.1.call-start = ((), (), s32[]{:S(2)}) async-start(), calls=%async_computation.5 | async-start | bytes 655360 | tf_op jit(solution)/shard_map/reduce_scatter | solution.py:135
  110.8 5.9 %copy-start.4 = (s32[4,64]{1,0:T(4,128)S(1)}, s32[4,64]{1,0:T(4,128)}, u32[]{:S(2)}) copy-start(s32[4,64]{1,0:T(4,128)} %param.14) | copy-start | bytes 3076
  110.8 5.9 %copy-start.1 = (bf16[2,256,1024]{2,0,1:T(2,128)(2,1)S(1)}, bf16[2,256,1024]{2,0,1:T(2,128)(2,1)}, u32[]{:S(2)}) copy-start(bf16[2,256,1024]{2,0,1:T(2,128)(2,1)} %all-gather.2.cloned.1.call-done) | copy-start | bytes 3145732
Sparse Core Ops, SparseCore 0:
  12.1 47.1 all-gather.1
  116.8 20.5 reduce-scatter.1
